TPU v7x, 32 devices: a whole 2x2x4 slice. The times are simulated.
32 devices in a mesh: view: 4 (over x, core), bx: 4 (over z), by: 2 (over y).
Axes of the slice: x: 2, y: 2, z: 4, core: 2. Of those that a mesh axis runs over, the one named last changes fastest.
Arguments:
- estimate: float32 [256, 32, 128], P('bx', 'by'), may hold values from 0.5 to 2
- observed: float32 [4, 2048, 512], P('view', ('bx', 'by')), may hold values from 0.25 to 4
- destination: int32 [4, 2048, 1], P('view', ('bx', 'by')), may hold values from 0 to 7; in each aligned block of 256 rows (0 to 255, 256 to 511, ..., all dimensions but the last counted through in order) at most 64 rows name the same one
- slot_index: int32 [4, 2048], P('view', ('bx', 'by')), may hold values from 0 to 255
- valid_count: int32 [4, 2048], P('view', ('bx', 'by')), may hold values from 32 to 128
- blend_weight: float32 [4, 2048], P('view', ('bx', 'by')), may hold values from 0.2 to 1
- kernel_x: float32 [4, 17], P('view'), may hold values from 0.1 to 1
- kernel_y: float32 [4, 17], P('view'), may hold values from 0.1 to 1
- kernel_z: float32 [4, 33], P('view'), may hold values from 0.1 to 1
Outputs:
- updated: float32 [256, 32, 128], P('bx', 'by')
Inputs may be any that keep to these rules, and one draw needn't show every extreme that they name: `destination`: in each view, the 256 rows of one device name no brick more than 64 times, a bound that some block reaches.
All inputs are finite; a program needn't handle non-finite values.
Results may differ from a plain program's by a relative error of at most 0.0001.
Values sent between devices are 32-bit elements; how exact they have to be, the bound alone decides.
No kernel may reach another device: no remote copies, remote signals or barrier semaphores. Data moves between devices by JAX's collectives and lax.ppermute only.
A program may use at most 64 MiB of HBM per device.

v0:
```python
import jax
import jax.numpy as jnp
from jax import lax
from jax.sharding import PartitionSpec as P

R = 8
RZ = 16
YP = 4
PV = 512
SLOTS = 256
PIECES = 256
PRIOR_WEIGHT = 0.5


def with_halo(block, sides, width):
    for axis, dim in sides:
        count = lax.axis_size(axis)
        forward = [(i, i + 1) for i in range(count - 1)]
        backward = [(target, source) for source, target in forward]
        low = lax.ppermute(
            lax.slice_in_dim(block, block.shape[dim] - width, None, axis=dim), axis, forward
        )
        high = lax.ppermute(lax.slice_in_dim(block, 0, width, axis=dim), axis, backward)
        block = jnp.concatenate([low, block, high], axis=dim)
    return block


def band_matrix(kernel, extent, radius):
    spread = jnp.arange(extent + 2 * radius)[None, :] - jnp.arange(extent)[:, None]
    offsets = jnp.arange(2 * radius + 1)
    hits = (spread[:, :, None] == offsets[None, None, :]).astype(jnp.float32)
    return jnp.sum(kernel[None, None, :] * hits, axis=2)


def separable(padded, kernel_a, kernel_b, kernel_c):
    rows_x = padded.shape[0] - 2 * R
    rows_y = padded.shape[1] - 2 * R
    depth_cells = padded.shape[2]
    along_first = jnp.einsum(
        "xe,eyz->xyz", band_matrix(kernel_a, rows_x, R), padded, precision=lax.Precision.HIGHEST
    )
    second = jnp.einsum(
        "ye,xez->xyz",
        band_matrix(kernel_b, rows_y, R),
        along_first,
        precision=lax.Precision.HIGHEST,
    )
    depth_band = band_matrix(kernel_c, depth_cells, RZ)[:, RZ : RZ + depth_cells]
    return jnp.einsum("zw,xyw->xyz", depth_band, second, precision=lax.Precision.HIGHEST)


def local(
    estimate,
    observed,
    destination,
    slot_index,
    valid_count,
    blend_weight,
    kernel_x,
    kernel_y,
    kernel_z,
):
    rows_x, rows_y, depth_cells = estimate.shape
    norm_x = kernel_x[0] / jnp.sum(kernel_x[0])
    norm_y = kernel_y[0] / jnp.sum(kernel_y[0])
    norm_z = kernel_z[0] / jnp.sum(kernel_z[0])
    padded = with_halo(estimate, (("bx", 0), ("by", 1)), R)
    blurred = separable(padded, norm_x, norm_y, norm_z)
    count_bx = lax.axis_size("bx")
    count_by = lax.axis_size("by")
    bricks = count_bx * count_by
    capacity = max(4, 2 * PIECES // bricks)
    target = destination[0, :, 0]
    member = (target[:, None] == jnp.arange(bricks)[None, :]).astype(jnp.int32)
    slot_rank = jnp.sum((jnp.cumsum(member, axis=0) - 1) * member, axis=1)
    send_place = target * capacity + slot_rank
    send_rows = jnp.zeros((bricks * capacity, PV), jnp.float32).at[send_place].set(observed[0])
    send_meta = (
        jnp.zeros((bricks * capacity, 2), jnp.int32)
        .at[send_place]
        .set(jnp.stack([slot_index[0], valid_count[0]], axis=1))
    )
    send_weight = jnp.zeros((bricks * capacity,), jnp.float32).at[send_place].set(blend_weight[0])
    recv_rows, recv_meta, recv_weight = (
        lax.all_to_all(
            send_rows.reshape(bricks, capacity, PV),
            ("bx", "by"),
            split_axis=0,
            concat_axis=0,
            tiled=True,
        ),
        lax.all_to_all(
            send_meta.reshape(bricks, capacity, 2),
            ("bx", "by"),
            split_axis=0,
            concat_axis=0,
            tiled=True,
        ),
        lax.all_to_all(
            send_weight.reshape(bricks, capacity),
            ("bx", "by"),
            split_axis=0,
            concat_axis=0,
            tiled=True,
        ),
    )
    recv_rows = recv_rows.reshape(bricks * capacity, PV)
    recv_meta = recv_meta.reshape(bricks * capacity, 2)
    recv_weight = recv_weight.reshape(bricks * capacity)
    depth_index = jnp.arange(depth_cells, dtype=jnp.int32)
    keep_mask = (depth_index[None, :] < recv_meta[:, 1:2]).astype(jnp.float32) * recv_weight[
        :, None
    ]
    weighted = (recv_rows.reshape(-1, YP, depth_cells) * keep_mask[:, None, :]).reshape(-1, PV)
    chooser = (jnp.arange(SLOTS)[:, None] == recv_meta[:, 0][None, :]).astype(jnp.float32)
    data_slots = jnp.dot(chooser, weighted, precision=lax.Precision.HIGHEST)
    cover_slots = jnp.dot(chooser, keep_mask, precision=lax.Precision.HIGHEST)
    data_volume = data_slots.reshape(rows_x, rows_y, depth_cells)
    cover_wide = jnp.broadcast_to(
        cover_slots.reshape(rows_x, rows_y // YP, 1, depth_cells),
        (rows_x, rows_y // YP, YP, depth_cells),
    )
    cover_volume = cover_wide.reshape(rows_x, rows_y, depth_cells)
    ratio_field = (data_volume + PRIOR_WEIGHT * blurred) / ((cover_volume + PRIOR_WEIGHT) * blurred)
    padded_ratio = with_halo(ratio_field, (("bx", 0), ("by", 1)), R)
    correction = separable(padded_ratio, norm_x[::-1], norm_y[::-1], norm_z[::-1])
    log_term = jnp.log(correction)
    logsum = lax.psum(log_term, "view")
    return estimate * jnp.exp(logsum)


def solution(mesh):
    placed = (
        P("bx", "by", None),
        P("view", ("bx", "by"), None),
        P("view", ("bx", "by"), None),
        P("view", ("bx", "by")),
        P("view", ("bx", "by")),
        P("view", ("bx", "by")),
        P("view", None),
        P("view", None),
        P("view", None),
    )
    return jax.shard_map(
        local, mesh=mesh, in_specs=placed, out_specs=P("bx", "by", None), check_vma=False
    )
```

profile of v0, /device:TPU:0, one launch (start us, length us, event | category | flops | bytes accessed | tf_op | source)
XLA Modules:
  0.0 148.1 jit_solution(831064255658808431)
XLA Ops:
  6.5 0.7 fusion.26
  8.1 0.8 fusion.23
  8.9 0.7 compare_select_fusion
  9.6 1.6 %scatter_custom_fusion.2 = f32[512]{0:T(512)S(1)} fusion(s32[256]{0:T(256)S(1)} %bitcast.81, f32[256]{0:T(256)} %bitcast.89, f32[]{:T(128)} %constant.22.clone.1), kind=kCustom, calls=%fused_computation.64 | custom fusion | bytes 2560 | tf_op jit(solution)/shard_map/scatter | solution.py:83
  11.1 0.7 all_to_all.14
  11.8 7.3 %all-to-all-start.2 = ((f32[8,1,64]{2,1,0:T(1,128)}), f32[8,1,64]{2,1,0:T(1,128)S(1)}, u32[]{:S(2)}, u32[]{:S(2)}) async-start(f32[8,1,64]{2,1,0:T(1,128)} %all_to_all.14), calls=%async_computation.2 | async-start | bytes 8192 | tf_op jit(solution)/shard_map/all_to_all | solution.py:99
  19.1 0.9 fusion.34
  20.0 3.9 %collective-permute-start = (f32[8,16,128]{2,0,1:T(8,128)S(1)}, f32[8,16,128]{2,0,1:T(8,128)S(1)}, u32[]{:S(2)}, u32[]{:S(2)}) collective-permute-start(f32[8,16,128]{2,0,1:T(8,128)S(1)} %copy.60), channel_id=1, source_target_pairs={{0,2},{2,4},{4,6},{1,3},{3,5},{5,7},{8,10},{10,12},{12,14},{9,11},... | collective-permute-start | bytes 196616 | tf_op jit(solution)/shard_map/ppermute | solution.py:20
  24.0 1.3 collective-permute-start.1
  25.3 1.3 reduce_sum.92
  26.6 0.7 reverse.9
  27.3 1.3 reduce_sum.97
  28.6 0.7 reverse.10
  29.3 1.3 reduce_sum.99
  30.6 0.7 reverse.11
  31.4 1.3 broadcast_divide_fusion.4
  32.7 1.2 broadcast_divide_fusion.2
  33.9 1.3 broadcast_divide_fusion
  36.0 0.7 pad_add_fusion
  36.8 1.2 scatter_custom_fusion
  38.2 0.7 reshape.213
  38.9 6.6 %all-to-all-start = ((s32[8,1,128]{2,1,0:T(1,128)}), s32[8,1,128]{2,1,0:T(1,128)S(1)}, u32[]{:S(2)}, u32[]{:S(2)}) async-start(s32[8,1,128]{2,1,0:T(1,128)} %reshape.213), calls=%async_computation | async-start | bytes 8192 | tf_op jit(solution)/shard_map/all_to_all | solution.py:92
  45.6 2.5 %scatter_custom_fusion.1 = f32[512,512]{1,0:T(8,128)} fusion(s32[256]{0:T(256)S(1)} %bitcast.83, f32[1,256,512]{2,1,0:T(8,128)S(1)} %copy-done, f32[]{:T(128)} %constant.22.clone.1), kind=kCustom, calls=%fused_computation.28 | custom fusion | bytes 1572868 | tf_op jit(solution)/shard_map/scatter | solution.py:77
  48.7 0.7 reduce.8
  49.5 2.5 %all-to-all-done = s32[8,1,128]{2,1,0:T(1,128)S(1)} async-done(((s32[8,1,128]{2,1,0:T(1,128)}), s32[8,1,128]{2,1,0:T(1,128)S(1)}, u32[]{:S(2)}, u32[]{:S(2)}) %all-to-all-start) | async-done | bytes 4128 | tf_op jit(solution)/shard_map/all_to_all | solution.py:92
  51.9 3.6 %all-to-all-start.1 = ((f32[8,64,512]{2,1,0:T(8,128)}), f32[8,64,512]{2,1,0:T(8,128)S(1)}, u32[]{:S(2)}, u32[]{:S(2)}) async-start(f32[8,64,512]{2,1,0:T(8,128)} %bitcast.14), calls=%async_computation.1 | async-start | bytes 2097152 | tf_op jit(solution)/shard_map/all_to_all | solution.py:85
  56.0 0.7 reduce.9
  57.1 3.9 %collective-permute-start.2 = (f32[80,8,128]{2,0,1:T(8,128)S(1)}, f32[80,8,128]{2,0,1:T(8,128)S(1)}, u32[]{:S(2)}, u32[]{:S(2)}) collective-permute-start(f32[80,8,128]{2,0,1:T(8,128)S(1)} %get-tuple-element.13), channel_id=1, source_target_pairs={{0,1},{2,3},{4,5},{6,7},{8,9},{10,11},{12,13},{14,15},{16,17},{18,... | collective-permute-start | bytes 983048 | tf_op jit(solution)/shard_map/ppermute | solution.py:20
  61.0 1.3 collective-permute-start.3
  63.1 7.8 %collective-permute-done.2 = f32[80,8,128]{2,0,1:T(8,128)S(1)} collective-permute-done((f32[80,8,128]{2,0,1:T(8,128)S(1)}, f32[80,8,128]{2,0,1:T(8,128)S(1)}, u32[]{:S(2)}, u32[]{:S(2)}) %collective-permute-start.2) | collective-permute-done | bytes 327712 | tf_op jit(solution)/shard_map/ppermute | solution.py:20
  70.8 4.3 %collective-permute-done.3 = f32[80,8,128]{2,0,1:T(8,128)S(1)} collective-permute-done((f32[80,8,128]{2,0,1:T(8,128)S(1)}, f32[80,8,128]{2,0,1:T(8,128)S(1)}, u32[]{:S(2)}, u32[]{:S(2)}) %collective-permute-start.3) | collective-permute-done | bytes 327712 | tf_op jit(solution)/shard_map/ppermute | solution.py:23
  75.2 1.0 fusion
  76.2 1.3 convolution_bitcast_fusion.1
  77.5 2.3 %all-to-all-done.1 = f32[8,64,512]{2,1,0:T(8,128)S(1)} async-done(((f32[8,64,512]{2,1,0:T(8,128)}), f32[8,64,512]{2,1,0:T(8,128)S(1)}, u32[]{:S(2)}, u32[]{:S(2)}) %all-to-all-start.1) | async-done | bytes 1048608 | tf_op jit(solution)/shard_map/all_to_all | solution.py:85
  79.9 0.7 fusion.8
  80.8 0.6 multiply_divide_fusion
  81.5 1.7 %collective-permute-start.4 = (f32[8,16,128]{2,1,0:T(8,128)S(1)}, f32[8,16,128]{2,1,0:T(8,128)S(1)}, u32[]{:S(2)}, u32[]{:S(2)}) collective-permute-start(f32[8,16,128]{2,1,0:T(8,128)S(1)} %get-tuple-element.15), channel_id=1, source_target_pairs={{0,2},{2,4},{4,6},{1,3},{3,5},{5,7},{8,10},{10,12},{12,14},{9,11},... | collective-permute-start | bytes 196616 | tf_op jit(solution)/shard_map/ppermute | solution.py:20
  83.2 1.3 collective-permute-start.5
  85.1 4.3 %collective-permute-done.5 = f32[8,16,128]{2,1,0:T(8,128)S(1)} collective-permute-done((f32[8,16,128]{2,1,0:T(8,128)S(1)}, f32[8,16,128]{2,1,0:T(8,128)S(1)}, u32[]{:S(2)}, u32[]{:S(2)}) %collective-permute-start.5) | collective-permute-done | bytes 65568 | tf_op jit(solution)/shard_map/ppermute | solution.py:23
  89.4 2.7 %collective-permute-start.6 = (f32[80,8,128]{2,1,0:T(8,128)S(1)}, f32[80,8,128]{2,1,0:T(8,128)S(1)}, u32[]{:S(2)}, u32[]{:S(2)}) collective-permute-start(f32[80,8,128]{2,1,0:T(8,128)S(1)} %get-tuple-element.11), channel_id=1, source_target_pairs={{0,1},{2,3},{4,5},{6,7},{8,9},{10,11},{12,13},{14,15},{16,17},{18,... | collective-permute-start | bytes 983048 | tf_op jit(solution)/shard_map/ppermute | solution.py:20
  92.2 1.5 collective-permute-start.7
  93.6 3.5 %collective-permute-done.6 = f32[80,8,128]{2,1,0:T(8,128)S(1)} collective-permute-done((f32[80,8,128]{2,1,0:T(8,128)S(1)}, f32[80,8,128]{2,1,0:T(8,128)S(1)}, u32[]{:S(2)}, u32[]{:S(2)}) %collective-permute-start.6) | collective-permute-done | bytes 327712 | tf_op jit(solution)/shard_map/ppermute | solution.py:20
  97.1 4.1 %collective-permute-done.7 = f32[80,8,128]{2,1,0:T(8,128)S(1)} collective-permute-done((f32[80,8,128]{2,1,0:T(8,128)S(1)}, f32[80,8,128]{2,1,0:T(8,128)S(1)}, u32[]{:S(2)}, u32[]{:S(2)}) %collective-permute-start.7) | collective-permute-done | bytes 327712 | tf_op jit(solution)/shard_map/ppermute | solution.py:23
  101.4 1.8 %fusion.6 = f32[64,32,128]{2,0,1:T(8,128)S(1)} fusion(f32[80,32,128]{2,1,0:T(8,128)S(1)} %pad_maximum_fusion, f32[64,80]{1,0:T(8,128)S(1)} %get-tuple-element.7), kind=kOutput, calls=%fused_computation.13 | convolution fusion | flops 251658240 | bytes 2379776 | tf_op jit(solution)/shard_map/xe,eyz->xyz/dot_general | solution.py:39
  103.1 1.3 convolution_bitcast_fusion
  104.4 1.4 convolution_log_fusion
  105.8 33.5 %all-reduce.2.cloned.1.call-done = f32[64,16,128]{2,1,0:T(8,128)} async-done(((f32[64,16,128]{2,1,0:T(8,128)}), f32[64,16,128]{2,1,0:T(8,128)}) %all-reduce.2.cloned.1.call-update) | async-done | bytes 524304 | tf_op jit(solution)/shard_map/psum | solution.py:128
  139.3 1.9 %exponential_multiply_fusion = f32[64,16,128]{2,1,0:T(8,128)} fusion(f32[64,16,128]{2,1,0:T(8,128)S(1)} %copy-done.1, f32[64,16,128]{2,1,0:T(8,128)} %all-reduce.2.cloned.1.call-done), kind=kLoop, calls=%fused_computation.30 | loop fusion | flops 131072 | bytes 1572864 | tf_op jit(solution)/shard_map/mul | solution.py:129
  (44 shorter events, 5.5 us)
Async XLA Ops:
  6.5 39.1 %copy-start = (f32[1,256,512]{2,1,0:T(8,128)S(1)}, f32[1,256,512]{2,1,0:T(8,128)}, u32[]{:S(2)}) copy-start(f32[1,256,512]{2,1,0:T(8,128)} %param.10) | copy-start | bytes 1572868
  11.8 27.1 %all-to-all-start.2 = ((f32[8,1,64]{2,1,0:T(1,128)}), f32[8,1,64]{2,1,0:T(1,128)S(1)}, u32[]{:S(2)}, u32[]{:S(2)}) async-start(f32[8,1,64]{2,1,0:T(1,128)} %all_to_all.14), calls=%async_computation.2 | async-start | bytes 8192 | tf_op jit(solution)/shard_map/all_to_all | solution.py:99
  20.0 36.9 %collective-permute-start = (f32[8,16,128]{2,0,1:T(8,128)S(1)}, f32[8,16,128]{2,0,1:T(8,128)S(1)}, u32[]{:S(2)}, u32[]{:S(2)}) collective-permute-start(f32[8,16,128]{2,0,1:T(8,128)S(1)} %copy.60), channel_id=1, source_target_pairs={{0,2},{2,4},{4,6},{1,3},{3,5},{5,7},{8,10},{10,12},{12,14},{9,11},... | collective-permute-start | bytes 196616 | tf_op jit(solution)/shard_map/ppermute | solution.py:20
  24.0 33.1 %collective-permute-start.1 = (f32[8,16,128]{2,0,1:T(8,128)S(1)}, f32[8,16,128]{2,0,1:T(8,128)S(1)}, u32[]{:S(2)}, u32[]{:S(2)}) collective-permute-start(f32[8,16,128]{2,0,1:T(8,128)S(1)} %copy.61), channel_id=1, source_target_pairs={{2,0},{4,2},{6,4},{3,1},{5,3},{7,5},{10,8},{12,10},{14,12},{11,9},... | collective-permute-start | bytes 196616 | tf_op jit(solution)/shard_map/ppermute | solution.py:23
  38.9 13.0 %all-to-all-start = ((s32[8,1,128]{2,1,0:T(1,128)}), s32[8,1,128]{2,1,0:T(1,128)S(1)}, u32[]{:S(2)}, u32[]{:S(2)}) async-start(s32[8,1,128]{2,1,0:T(1,128)} %reshape.213), calls=%async_computation | async-start | bytes 8192 | tf_op jit(solution)/shard_map/all_to_all | solution.py:92
  48.1 8.8 %copy-start.1 = (f32[64,16,128]{2,1,0:T(8,128)S(1)}, f32[64,16,128]{2,1,0:T(8,128)}, u32[]{:S(2)}) copy-start(f32[64,16,128]{2,1,0:T(8,128)} %param.9) | copy-start | bytes 1572868
  51.9 27.9 %all-to-all-start.1 = ((f32[8,64,512]{2,1,0:T(8,128)}), f32[8,64,512]{2,1,0:T(8,128)S(1)}, u32[]{:S(2)}, u32[]{:S(2)}) async-start(f32[8,64,512]{2,1,0:T(8,128)} %bitcast.14), calls=%async_computation.1 | async-start | bytes 2097152 | tf_op jit(solution)/shard_map/all_to_all | solution.py:85
  55.5 83.9 %all-reduce.2.cloned.1.call-start = ((), (), s32[]{:S(2)}) async-start(), calls=%async_computation.3 | async-start | bytes 1048576 | tf_op jit(solution)/shard_map/psum | solution.py:128
  57.1 13.7 %collective-permute-start.2 = (f32[80,8,128]{2,0,1:T(8,128)S(1)}, f32[80,8,128]{2,0,1:T(8,128)S(1)}, u32[]{:S(2)}, u32[]{:S(2)}) collective-permute-start(f32[80,8,128]{2,0,1:T(8,128)S(1)} %get-tuple-element.13), channel_id=1, source_target_pairs={{0,1},{2,3},{4,5},{6,7},{8,9},{10,11},{12,13},{14,15},{16,17},{18,... | collective-permute-start | bytes 983048 | tf_op jit(solution)/shard_map/ppermute | solution.py:20
  61.0 14.1 %collective-permute-start.3 = (f32[80,8,128]{2,0,1:T(8,128)S(1)}, f32[80,8,128]{2,0,1:T(8,128)S(1)}, u32[]{:S(2)}, u32[]{:S(2)}) collective-permute-start(f32[80,8,128]{2,0,1:T(8,128)S(1)} %get-tuple-element.14), channel_id=1, source_target_pairs={{1,0},{3,2},{5,4},{7,6},{9,8},{11,10},{13,12},{15,14},{17,16},{19,... | collective-permute-start | bytes 983048 | tf_op jit(solution)/shard_map/ppermute | solution.py:23
  81.5 3.6 %collective-permute-start.4 = (f32[8,16,128]{2,1,0:T(8,128)S(1)}, f32[8,16,128]{2,1,0:T(8,128)S(1)}, u32[]{:S(2)}, u32[]{:S(2)}) collective-permute-start(f32[8,16,128]{2,1,0:T(8,128)S(1)} %get-tuple-element.15), channel_id=1, source_target_pairs={{0,2},{2,4},{4,6},{1,3},{3,5},{5,7},{8,10},{10,12},{12,14},{9,11},... | collective-permute-start | bytes 196616 | tf_op jit(solution)/shard_map/ppermute | solution.py:20
  83.2 6.2 %collective-permute-start.5 = (f32[8,16,128]{2,1,0:T(8,128)S(1)}, f32[8,16,128]{2,1,0:T(8,128)S(1)}, u32[]{:S(2)}, u32[]{:S(2)}) collective-permute-start(f32[8,16,128]{2,1,0:T(8,128)S(1)} %get-tuple-element.16), channel_id=1, source_target_pairs={{2,0},{4,2},{6,4},{3,1},{5,3},{7,5},{10,8},{12,10},{14,12},{11,9},... | collective-permute-start | bytes 196616 | tf_op jit(solution)/shard_map/ppermute | solution.py:23
  89.4 7.7 %collective-permute-start.6 = (f32[80,8,128]{2,1,0:T(8,128)S(1)}, f32[80,8,128]{2,1,0:T(8,128)S(1)}, u32[]{:S(2)}, u32[]{:S(2)}) collective-permute-start(f32[80,8,128]{2,1,0:T(8,128)S(1)} %get-tuple-element.11), channel_id=1, source_target_pairs={{0,1},{2,3},{4,5},{6,7},{8,9},{10,11},{12,13},{14,15},{16,17},{18,... | collective-permute-start | bytes 983048 | tf_op jit(solution)/shard_map/ppermute | solution.py:20
  92.2 9.1 %collective-permute-start.7 = (f32[80,8,128]{2,1,0:T(8,128)S(1)}, f32[80,8,128]{2,1,0:T(8,128)S(1)}, u32[]{:S(2)}, u32[]{:S(2)}) collective-permute-start(f32[80,8,128]{2,1,0:T(8,128)S(1)} %get-tuple-element.12), channel_id=1, source_target_pairs={{1,0},{3,2},{5,4},{7,6},{9,8},{11,10},{13,12},{15,14},{17,16},{19,... | collective-permute-start | bytes 983048 | tf_op jit(solution)/shard_map/ppermute | solution.py:23
Sparse Core Ops, SparseCore 0:
  105.9 33.3 all-reduce.1
where the time goes:
time: 149 us; the launch traced here: 148 us
  waiting for transfers between devices  62.8 us (42%)
  starting transfers between devices  35.1 us (24%)
  other arithmetic  15.7 us (11%)
  between operations  13.7 us (9%)
  local copies, waits for them, and re-layouts  12.2 us (8%)
  matrix products  8.59 us (6%)
    psum x1, waiting for transfers between devices, local(): logsum = lax.psum(log_term, 'view')  33.5 us
    ppermute x4, waiting for transfers between devices, with_halo(): lax.ppermute(lax.slice_in_dim(block, 0, width, axis=dim), axis, backward)  12.7 us
    ppermute x4, starting transfers between devices, with_halo(): lax.ppermute(lax.slice_in_dim(block, block.shape[dim] - width, None, axis...  12.2 us
    ppermute x4, waiting for transfers between devices, with_halo(): lax.ppermute(lax.slice_in_dim(block, block.shape[dim] - width, None, axis...  11.8 us
    all_to_all x1, starting transfers between devices, local(): lax.all_to_all(send_weight.reshape(bricks, capacity), ('bx', 'by'), split...  7.31 us
    all_to_all x1, starting transfers between devices, local(): lax.all_to_all(send_meta.reshape(bricks, capacity, 2), ('bx', 'by'), spli...  6.62 us
    ppermute x4, starting transfers between devices, with_halo(): lax.ppermute(lax.slice_in_dim(block, 0, width, axis=dim), axis, backward)  5.35 us
    all_to_all x1, starting transfers between devices, local(): lax.all_to_all(send_rows.reshape(bricks, capacity, PV), ('bx', 'by'), spl...  3.56 us
  transfers between devices with their start and end apart: 12, of which 9 were waited for; matrix products, arithmetic and copies ran while one was open for 16% of the time, Pallas kernels for 0%

commit v1 on v0

--- a/solution.py
+++ b/solution.py
@@ -10,6 +10,27 @@
 SLOTS = 256
 PIECES = 256
 PRIOR_WEIGHT = 0.5
+
+
+def _plan_ranges(mine_x):
+    named_axis = ("bx", "by")
+    left_arr = lax.axis_size(named_axis)
+    wide_out = lax.axis_index(named_axis)
+    known, moved = (left_arr, wide_out)
+    b_next = mine_x.shape[0] // known
+    e_now = list(mine_x.shape)
+    e_now[0] = b_next
+    v_next = e_now[0]
+    e_now[0] = v_next * known
+    mid_arr = jnp.zeros(e_now, mine_x.dtype)
+    for src_i in [*range(known)]:
+        y1 = lax.dynamic_slice_in_dim(mine_x, (moved ^ src_i) * b_next, b_next, axis=0)
+        if src_i:
+            y1 = lax.ppermute(
+                y1, axis_name=named_axis, perm=[(dd, dd ^ src_i) for dd in range(known)]
+            )
+        mid_arr = lax.dynamic_update_slice_in_dim(mid_arr, y1, (moved ^ src_i) * v_next, axis=0)
+    return mid_arr
 
 
 def with_halo(block, sides, width):
@@ -89,13 +110,7 @@
             concat_axis=0,
             tiled=True,
         ),
-        lax.all_to_all(
-            send_meta.reshape(bricks, capacity, 2),
-            ("bx", "by"),
-            split_axis=0,
-            concat_axis=0,
-            tiled=True,
-        ),
+        _plan_ranges(send_meta.reshape(bricks, capacity, 2)),
         lax.all_to_all(
             send_weight.reshape(bricks, capacity),
             ("bx", "by"),

time: 149 us -> 143 us (0.960)
  starting transfers between devices: 35.1 us -> 41 us
  other arithmetic: 15.7 us -> 11.1 us
  local copies, waits for them, and re-layouts: 12.2 us -> 8.69 us
  waiting for transfers between devices: 62.8 us -> 59.4 us
    ppermute x0 -> x7, starting transfers between devices: none -> 14.3 us  [_plan_ranges(): lax.ppermute(y1, axis_name=named_axis, perm=[(dd, dd ^ src_i) for dd in r...]
    ppermute x4, waiting for transfers between devices: 11.8 us -> 3.66 us  [with_halo(): lax.ppermute(lax.slice_in_dim(block, block.shape[dim] - width, None, axis...]
    all_to_all x1 -> x0, starting transfers between devices: 6.62 us -> none  [local(): lax.all_to_all(send_meta.reshape(bricks, capacity, 2), ('bx', 'by'), spli...]
    ppermute x4, waiting for transfers between devices: 12.7 us -> 18.9 us  [with_halo(): lax.ppermute(lax.slice_in_dim(block, 0, width, axis=dim), axis, backward)]
    all_to_all x1 -> x0, waiting for transfers between devices: 2.46 us -> none  [local(): lax.all_to_all(send_meta.reshape(bricks, capacity, 2), ('bx', 'by'), spli...]
    all_to_all x1, starting transfers between devices: 7.31 us -> 4.88 us  [local(): lax.all_to_all(send_weight.reshape(bricks, capacity), ('bx', 'by'), split...]
    all_to_all x1, starting transfers between devices: 3.56 us -> 5.8 us  [local(): lax.all_to_all(send_rows.reshape(bricks, capacity, PV), ('bx', 'by'), spl...]
    another operation x4, local copies, waits for them, and re-layouts: 2.24 us -> 0.29 us
  transfers between devices with their start and end apart: 12 -> 18, of which waited for: 9 -> 8; matrix products, arithmetic and copies ran while one was open for 16% -> 10% of each run, Pallas kernels for 0% -> 0%
where the time goes in v1:
time: 143 us
  waiting for transfers between devices  59.4 us (42%)
  starting transfers between devices  41 us (29%)
  between operations  13.9 us (10%)
  other arithmetic  11.1 us (8%)
  local copies, waits for them, and re-layouts  8.69 us (6%)
  matrix products  8.59 us (6%)
    psum x1, waiting for transfers between devices, local(): logsum = lax.psum(log_term, 'view')  32.9 us
    ppermute x4, waiting for transfers between devices, with_halo(): lax.ppermute(lax.slice_in_dim(block, 0, width, axis=dim), axis, backward)  18.9 us
    ppermute x7, starting transfers between devices, _plan_ranges(): lax.ppermute(y1, axis_name=named_axis, perm=[(dd, dd ^ src_i) for dd in r...  14.3 us
    ppermute x4, starting transfers between devices, with_halo(): lax.ppermute(lax.slice_in_dim(block, block.shape[dim] - width, None, axis...  10.6 us
    all_to_all x1, starting transfers between devices, local(): lax.all_to_all(send_rows.reshape(bricks, capacity, PV), ('bx', 'by'), spl...  5.8 us
    ppermute x4, starting transfers between devices, with_halo(): lax.ppermute(lax.slice_in_dim(block, 0, width, axis=dim), axis, backward)  5.35 us
    all_to_all x1, starting transfers between devices, local(): lax.all_to_all(send_weight.reshape(bricks, capacity), ('bx', 'by'), split...  4.88 us
    ppermute x4, waiting for transfers between devices, with_halo(): lax.ppermute(lax.slice_in_dim(block, block.shape[dim] - width, None, axis...  3.66 us
  transfers between devices with their start and end apart: 18, of which 8 were waited for; matrix products, arithmetic and copies ran while one was open for 10% of the time, Pallas kernels for 0%

profile of v1, /device:TPU:0, one launch (start us, length us, event | category | flops | bytes accessed | tf_op | source)
XLA Modules:
  0.0 142.7 jit_solution(4774548977951901644)
XLA Ops:
  6.6 0.8 fusion.26
  7.3 0.6 reduce-window.6
  8.2 0.8 fusion.23
  8.9 0.7 compare_select_fusion
  9.6 0.7 pad_add_fusion
  10.5 1.2 scatter_custom_fusion
  11.8 3.1 %collective-permute-start = (s32[1,64,2]{2,1,0:T(8,128)S(1)}, s32[1,64,2]{2,1,0:T(8,128)S(1)}, u32[]{:S(2)}, u32[]{:S(2)}) collective-permute-start(s32[1,64,2]{2,1,0:T(8,128)S(1)} %get-tuple-element.25), channel_id=1, source_target_pairs={{0,1},{1,0},{2,3},{3,2},{4,5},{5,4},{6,7},{7,6},{8,9},{9,8},{10,11... | collective-permute-start | bytes 1544 | tf_op jit(solution)/shard_map/ppermute | solution.py:29
  14.8 1.6 %collective-permute-start.1 = (s32[1,64,2]{2,1,0:T(8,128)S(1)}, s32[1,64,2]{2,1,0:T(8,128)S(1)}, u32[]{:S(2)}, u32[]{:S(2)}) collective-permute-start(s32[1,64,2]{2,1,0:T(8,128)S(1)} %get-tuple-element.24), channel_id=1, source_target_pairs={{0,2},{1,3},{2,0},{3,1},{4,6},{5,7},{6,4},{7,5},{8,10},{9,11},{10,... | collective-permute-start | bytes 1544 | tf_op jit(solution)/shard_map/ppermute | solution.py:29
  16.4 3.0 %collective-permute-start.3 = (s32[1,64,2]{2,1,0:T(8,128)S(1)}, s32[1,64,2]{2,1,0:T(8,128)S(1)}, u32[]{:S(2)}, u32[]{:S(2)}) collective-permute-start(s32[1,64,2]{2,1,0:T(8,128)S(1)} %get-tuple-element.22), channel_id=1, source_target_pairs={{0,4},{1,5},{2,6},{3,7},{4,0},{5,1},{6,2},{7,3},{8,12},{9,13},{10,... | collective-permute-start | bytes 1544 | tf_op jit(solution)/shard_map/ppermute | solution.py:29
  19.4 1.3 collective-permute-start.4
  20.7 1.6 %scatter_custom_fusion.2 = f32[512]{0:T(512)S(1)} fusion(s32[256]{0:T(256)S(1)} %bitcast.78, f32[256]{0:T(256)} %bitcast.85, f32[]{:T(128)} %constant.16.clone.1), kind=kCustom, calls=%fused_computation.72 | custom fusion | bytes 2560 | tf_op jit(solution)/shard_map/scatter | solution.py:104
  22.3 0.7 all_to_all.10
  22.9 4.9 %all-to-all-start.1 = ((f32[8,1,64]{2,1,0:T(1,128)}), f32[8,1,64]{2,1,0:T(1,128)S(1)}, u32[]{:S(2)}, u32[]{:S(2)}) async-start(f32[8,1,64]{2,1,0:T(1,128)} %all_to_all.10), calls=%async_computation.1 | async-start | bytes 8192 | tf_op jit(solution)/shard_map/all_to_all | solution.py:114
  27.9 0.7 reduce_sum.92
  28.7 0.6 reduce_sum.97
  29.4 0.6 reduce_sum.99
  30.1 0.7 broadcast_divide_fusion.4
  30.8 0.6 broadcast_divide_fusion.2
  31.4 0.6 broadcast_divide_fusion
  32.9 2.5 %scatter_custom_fusion.1 = f32[512,512]{1,0:T(8,128)} fusion(s32[256]{0:T(256)S(1)} %bitcast.79, f32[1,256,512]{2,1,0:T(8,128)S(1)} %copy-done, f32[]{:T(128)} %constant.16.clone.1), kind=kCustom, calls=%fused_computation.28 | custom fusion | bytes 1572868 | tf_op jit(solution)/shard_map/scatter | solution.py:98
  35.5 3.9 %collective-permute-start.5 = (s32[1,64,2]{2,1,0:T(8,128)S(1)}, s32[1,64,2]{2,1,0:T(8,128)S(1)}, u32[]{:S(2)}, u32[]{:S(2)}) collective-permute-start(s32[1,64,2]{2,1,0:T(8,128)S(1)} %get-tuple-element.20), channel_id=1, source_target_pairs={{0,6},{1,7},{2,4},{3,5},{4,2},{5,3},{6,0},{7,1},{8,14},{9,15},{10,... | collective-permute-start | bytes 1544 | tf_op jit(solution)/shard_map/ppermute | solution.py:29
  39.5 1.5 %collective-permute-start.6 = (s32[1,64,2]{2,1,0:T(8,128)S(1)}, s32[1,64,2]{2,1,0:T(8,128)S(1)}, u32[]{:S(2)}, u32[]{:S(2)}) collective-permute-start(s32[1,64,2]{2,1,0:T(8,128)S(1)} %get-tuple-element.19), channel_id=1, source_target_pairs={{0,7},{1,6},{2,5},{3,4},{4,3},{5,2},{6,1},{7,0},{8,15},{9,14},{10,... | collective-permute-start | bytes 1544 | tf_op jit(solution)/shard_map/ppermute | solution.py:29
  41.2 1.6 %collective-permute-start.7 = (f32[8,16,128]{2,0,1:T(8,128)S(1)}, f32[8,16,128]{2,0,1:T(8,128)S(1)}, u32[]{:S(2)}, u32[]{:S(2)}) collective-permute-start(f32[8,16,128]{2,0,1:T(8,128)S(1)} %copy.56), channel_id=1, source_target_pairs={{0,2},{2,4},{4,6},{1,3},{3,5},{5,7},{8,10},{10,12},{12,14},{9,11},... | collective-permute-start | bytes 196616 | tf_op jit(solution)/shard_map/ppermute | solution.py:41
  42.8 1.3 collective-permute-start.8
  44.5 1.7 %collective-permute-done.6 = s32[1,64,2]{2,1,0:T(8,128)S(1)} collective-permute-done((s32[1,64,2]{2,1,0:T(8,128)S(1)}, s32[1,64,2]{2,1,0:T(8,128)S(1)}, u32[]{:S(2)}, u32[]{:S(2)}) %collective-permute-start.6) | collective-permute-done | bytes 544 | tf_op jit(solution)/shard_map/ppermute | solution.py:29
  46.4 5.8 %all-to-all-start = ((f32[8,64,512]{2,1,0:T(8,128)}), f32[8,64,512]{2,1,0:T(8,128)S(1)}, u32[]{:S(2)}, u32[]{:S(2)}) async-start(f32[8,64,512]{2,1,0:T(8,128)} %bitcast.14), calls=%async_computation | async-start | bytes 2097152 | tf_op jit(solution)/shard_map/all_to_all | solution.py:106
  52.8 0.7 reduce.8
  53.8 1.3 collective-permute-start.10
  55.1 4.6 %collective-permute-start.9 = (f32[80,8,128]{2,0,1:T(8,128)S(1)}, f32[80,8,128]{2,0,1:T(8,128)S(1)}, u32[]{:S(2)}, u32[]{:S(2)}) collective-permute-start(f32[80,8,128]{2,0,1:T(8,128)S(1)} %get-tuple-element.13), channel_id=1, source_target_pairs={{0,1},{2,3},{4,5},{6,7},{8,9},{10,11},{12,13},{14,15},{16,17},{18,... | collective-permute-start | bytes 983048 | tf_op jit(solution)/shard_map/ppermute | solution.py:41
  60.4 10.2 %collective-permute-done.10 = f32[80,8,128]{2,0,1:T(8,128)S(1)} collective-permute-done((f32[80,8,128]{2,0,1:T(8,128)S(1)}, f32[80,8,128]{2,0,1:T(8,128)S(1)}, u32[]{:S(2)}, u32[]{:S(2)}) %collective-permute-start.10) | collective-permute-done | bytes 327712 | tf_op jit(solution)/shard_map/ppermute | solution.py:44
  70.6 1.0 fusion
  71.6 1.3 convolution_bitcast_fusion.1
  72.9 2.2 %all-to-all-done = f32[8,64,512]{2,1,0:T(8,128)S(1)} async-done(((f32[8,64,512]{2,1,0:T(8,128)}), f32[8,64,512]{2,1,0:T(8,128)S(1)}, u32[]{:S(2)}, u32[]{:S(2)}) %all-to-all-start) | async-done | bytes 1048608 | tf_op jit(solution)/shard_map/all_to_all | solution.py:106
  75.3 0.7 fusion.8
  76.2 0.6 multiply_divide_fusion
  76.8 1.7 %collective-permute-start.11 = (f32[8,16,128]{2,1,0:T(8,128)S(1)}, f32[8,16,128]{2,1,0:T(8,128)S(1)}, u32[]{:S(2)}, u32[]{:S(2)}) collective-permute-start(f32[8,16,128]{2,1,0:T(8,128)S(1)} %get-tuple-element.15), channel_id=1, source_target_pairs={{0,2},{2,4},{4,6},{1,3},{3,5},{5,7},{8,10},{10,12},{12,14},{9,11},... | collective-permute-start | bytes 196616 | tf_op jit(solution)/shard_map/ppermute | solution.py:41
  78.5 1.3 collective-permute-start.12
  79.8 0.6 collective-permute-done.11
  80.4 4.3 %collective-permute-done.12 = f32[8,16,128]{2,1,0:T(8,128)S(1)} collective-permute-done((f32[8,16,128]{2,1,0:T(8,128)S(1)}, f32[8,16,128]{2,1,0:T(8,128)S(1)}, u32[]{:S(2)}, u32[]{:S(2)}) %collective-permute-start.12) | collective-permute-done | bytes 65568 | tf_op jit(solution)/shard_map/ppermute | solution.py:44
  84.8 2.7 %collective-permute-start.13 = (f32[80,8,128]{2,1,0:T(8,128)S(1)}, f32[80,8,128]{2,1,0:T(8,128)S(1)}, u32[]{:S(2)}, u32[]{:S(2)}) collective-permute-start(f32[80,8,128]{2,1,0:T(8,128)S(1)} %get-tuple-element.11), channel_id=1, source_target_pairs={{0,1},{2,3},{4,5},{6,7},{8,9},{10,11},{12,13},{14,15},{16,17},{18,... | collective-permute-start | bytes 983048 | tf_op jit(solution)/shard_map/ppermute | solution.py:41
  87.5 1.5 %collective-permute-start.14 = (f32[80,8,128]{2,1,0:T(8,128)S(1)}, f32[80,8,128]{2,1,0:T(8,128)S(1)}, u32[]{:S(2)}, u32[]{:S(2)}) collective-permute-start(f32[80,8,128]{2,1,0:T(8,128)S(1)} %get-tuple-element.12), channel_id=1, source_target_pairs={{1,0},{3,2},{5,4},{7,6},{9,8},{11,10},{13,12},{15,14},{17,16},{19,... | collective-permute-start | bytes 983048 | tf_op jit(solution)/shard_map/ppermute | solution.py:44
  89.0 3.1 %collective-permute-done.13 = f32[80,8,128]{2,1,0:T(8,128)S(1)} collective-permute-done((f32[80,8,128]{2,1,0:T(8,128)S(1)}, f32[80,8,128]{2,1,0:T(8,128)S(1)}, u32[]{:S(2)}, u32[]{:S(2)}) %collective-permute-start.13) | collective-permute-done | bytes 327712 | tf_op jit(solution)/shard_map/ppermute | solution.py:41
  92.0 4.4 %collective-permute-done.14 = f32[80,8,128]{2,1,0:T(8,128)S(1)} collective-permute-done((f32[80,8,128]{2,1,0:T(8,128)S(1)}, f32[80,8,128]{2,1,0:T(8,128)S(1)}, u32[]{:S(2)}, u32[]{:S(2)}) %collective-permute-start.14) | collective-permute-done | bytes 327712 | tf_op jit(solution)/shard_map/ppermute | solution.py:44
  96.6 1.8 %fusion.6 = f32[64,32,128]{2,0,1:T(8,128)S(1)} fusion(f32[80,32,128]{2,1,0:T(8,128)S(1)} %pad_maximum_fusion, f32[64,80]{1,0:T(8,128)S(1)} %get-tuple-element.7), kind=kOutput, calls=%fused_computation.13 | convolution fusion | flops 251658240 | bytes 2379776 | tf_op jit(solution)/shard_map/xe,eyz->xyz/dot_general | solution.py:60
  98.3 1.3 convolution_bitcast_fusion
  99.6 1.4 convolution_log_fusion
  101.0 32.9 %all-reduce.2.cloned.1.call-done = f32[64,16,128]{2,1,0:T(8,128)} async-done(((f32[64,16,128]{2,1,0:T(8,128)}), f32[64,16,128]{2,1,0:T(8,128)}) %all-reduce.2.cloned.1.call-update) | async-done | bytes 524304 | tf_op jit(solution)/shard_map/psum | solution.py:143
  133.9 1.9 %exponential_multiply_fusion = f32[64,16,128]{2,1,0:T(8,128)} fusion(f32[64,16,128]{2,1,0:T(8,128)S(1)} %copy-done.1, f32[64,16,128]{2,1,0:T(8,128)} %all-reduce.2.cloned.1.call-done), kind=kLoop, calls=%fused_computation.30 | loop fusion | flops 131072 | bytes 1572864 | tf_op jit(solution)/shard_map/mul | solution.py:144
  (74 shorter events, 4.7 us)
Async XLA Ops:
  6.5 26.4 %copy-start = (f32[1,256,512]{2,1,0:T(8,128)S(1)}, f32[1,256,512]{2,1,0:T(8,128)}, u32[]{:S(2)}) copy-start(f32[1,256,512]{2,1,0:T(8,128)} %param.10) | copy-start | bytes 1572868
  6.5 21.3 %copy-start.1 = (f32[64,16,128]{2,1,0:T(8,128)S(1)}, f32[64,16,128]{2,1,0:T(8,128)}, u32[]{:S(2)}) copy-start(f32[64,16,128]{2,1,0:T(8,128)} %param.9) | copy-start | bytes 1572868
  6.5 21.3 %copy-start.2 = (f32[1,17]{1,0:T(1,128)S(1)}, f32[1,17]{1,0:T(1,128)}, u32[]{:S(2)}) copy-start(f32[1,17]{1,0:T(1,128)} %param.15) | copy-start | bytes 208
  6.5 22.1 %copy-start.3 = (f32[1,17]{1,0:T(1,128)S(1)}, f32[1,17]{1,0:T(1,128)}, u32[]{:S(2)}) copy-start(f32[1,17]{1,0:T(1,128)} %param.16) | copy-start | bytes 208
  6.5 22.8 %copy-start.4 = (f32[1,33]{1,0:T(1,128)S(1)}, f32[1,33]{1,0:T(1,128)}, u32[]{:S(2)}) copy-start(f32[1,33]{1,0:T(1,128)} %param.17) | copy-start | bytes 400
  11.8 23.7 %collective-permute-start = (s32[1,64,2]{2,1,0:T(8,128)S(1)}, s32[1,64,2]{2,1,0:T(8,128)S(1)}, u32[]{:S(2)}, u32[]{:S(2)}) collective-permute-start(s32[1,64,2]{2,1,0:T(8,128)S(1)} %get-tuple-element.25), channel_id=1, source_target_pairs={{0,1},{1,0},{2,3},{3,2},{4,5},{5,4},{6,7},{7,6},{8,9},{9,8},{10,11... | collective-permute-start | bytes 1544 | tf_op jit(solution)/shard_map/ppermute | solution.py:29
  14.8 24.7 %collective-permute-start.1 = (s32[1,64,2]{2,1,0:T(8,128)S(1)}, s32[1,64,2]{2,1,0:T(8,128)S(1)}, u32[]{:S(2)}, u32[]{:S(2)}) collective-permute-start(s32[1,64,2]{2,1,0:T(8,128)S(1)} %get-tuple-element.24), channel_id=1, source_target_pairs={{0,2},{1,3},{2,0},{3,1},{4,6},{5,7},{6,4},{7,5},{8,10},{9,11},{10,... | collective-permute-start | bytes 1544 | tf_op jit(solution)/shard_map/ppermute | solution.py:29
  16.4 24.7 %collective-permute-start.2 = (s32[1,64,2]{2,1,0:T(8,128)S(1)}, s32[1,64,2]{2,1,0:T(8,128)S(1)}, u32[]{:S(2)}, u32[]{:S(2)}) collective-permute-start(s32[1,64,2]{2,1,0:T(8,128)S(1)} %get-tuple-element.23), channel_id=1, source_target_pairs={{0,3},{1,2},{2,1},{3,0},{4,7},{5,6},{6,5},{7,4},{8,11},{9,10},{10,... | collective-permute-start | bytes 1544 | tf_op jit(solution)/shard_map/ppermute | solution.py:29
  16.4 26.4 %collective-permute-start.3 = (s32[1,64,2]{2,1,0:T(8,128)S(1)}, s32[1,64,2]{2,1,0:T(8,128)S(1)}, u32[]{:S(2)}, u32[]{:S(2)}) collective-permute-start(s32[1,64,2]{2,1,0:T(8,128)S(1)} %get-tuple-element.22), channel_id=1, source_target_pairs={{0,4},{1,5},{2,6},{3,7},{4,0},{5,1},{6,2},{7,3},{8,12},{9,13},{10,... | collective-permute-start | bytes 1544 | tf_op jit(solution)/shard_map/ppermute | solution.py:29
  19.4 24.8 %collective-permute-start.4 = (s32[1,64,2]{2,1,0:T(8,128)S(1)}, s32[1,64,2]{2,1,0:T(8,128)S(1)}, u32[]{:S(2)}, u32[]{:S(2)}) collective-permute-start(s32[1,64,2]{2,1,0:T(8,128)S(1)} %get-tuple-element.21), channel_id=1, source_target_pairs={{0,5},{1,4},{2,7},{3,6},{4,1},{5,0},{6,3},{7,2},{8,13},{9,12},{10,... | collective-permute-start | bytes 1544 | tf_op jit(solution)/shard_map/ppermute | solution.py:29
  22.9 23.5 %all-to-all-start.1 = ((f32[8,1,64]{2,1,0:T(1,128)}), f32[8,1,64]{2,1,0:T(1,128)S(1)}, u32[]{:S(2)}, u32[]{:S(2)}) async-start(f32[8,1,64]{2,1,0:T(1,128)} %all_to_all.10), calls=%async_computation.1 | async-start | bytes 8192 | tf_op jit(solution)/shard_map/all_to_all | solution.py:114
  35.5 8.8 %collective-permute-start.5 = (s32[1,64,2]{2,1,0:T(8,128)S(1)}, s32[1,64,2]{2,1,0:T(8,128)S(1)}, u32[]{:S(2)}, u32[]{:S(2)}) collective-permute-start(s32[1,64,2]{2,1,0:T(8,128)S(1)} %get-tuple-element.20), channel_id=1, source_target_pairs={{0,6},{1,7},{2,4},{3,5},{4,2},{5,3},{6,0},{7,1},{8,14},{9,15},{10,... | collective-permute-start | bytes 1544 | tf_op jit(solution)/shard_map/ppermute | solution.py:29
  39.5 6.7 %collective-permute-start.6 = (s32[1,64,2]{2,1,0:T(8,128)S(1)}, s32[1,64,2]{2,1,0:T(8,128)S(1)}, u32[]{:S(2)}, u32[]{:S(2)}) collective-permute-start(s32[1,64,2]{2,1,0:T(8,128)S(1)} %get-tuple-element.19), channel_id=1, source_target_pairs={{0,7},{1,6},{2,5},{3,4},{4,3},{5,2},{6,1},{7,0},{8,15},{9,14},{10,... | collective-permute-start | bytes 1544 | tf_op jit(solution)/shard_map/ppermute | solution.py:29
  41.2 12.3 %collective-permute-start.7 = (f32[8,16,128]{2,0,1:T(8,128)S(1)}, f32[8,16,128]{2,0,1:T(8,128)S(1)}, u32[]{:S(2)}, u32[]{:S(2)}) collective-permute-start(f32[8,16,128]{2,0,1:T(8,128)S(1)} %copy.56), channel_id=1, source_target_pairs={{0,2},{2,4},{4,6},{1,3},{3,5},{5,7},{8,10},{10,12},{12,14},{9,11},... | collective-permute-start | bytes 196616 | tf_op jit(solution)/shard_map/ppermute | solution.py:41
  42.8 10.8 %collective-permute-start.8 = (f32[8,16,128]{2,0,1:T(8,128)S(1)}, f32[8,16,128]{2,0,1:T(8,128)S(1)}, u32[]{:S(2)}, u32[]{:S(2)}) collective-permute-start(f32[8,16,128]{2,0,1:T(8,128)S(1)} %copy.57), channel_id=1, source_target_pairs={{2,0},{4,2},{6,4},{3,1},{5,3},{7,5},{10,8},{12,10},{14,12},{11,9},... | collective-permute-start | bytes 196616 | tf_op jit(solution)/shard_map/ppermute | solution.py:44
  46.4 28.7 %all-to-all-start = ((f32[8,64,512]{2,1,0:T(8,128)}), f32[8,64,512]{2,1,0:T(8,128)S(1)}, u32[]{:S(2)}, u32[]{:S(2)}) async-start(f32[8,64,512]{2,1,0:T(8,128)} %bitcast.14), calls=%async_computation | async-start | bytes 2097152 | tf_op jit(solution)/shard_map/all_to_all | solution.py:106
  52.2 81.7 %all-reduce.2.cloned.1.call-start = ((), (), s32[]{:S(2)}) async-start(), calls=%async_computation.2 | async-start | bytes 1048576 | tf_op jit(solution)/shard_map/psum | solution.py:143
  53.8 16.8 %collective-permute-start.10 = (f32[80,8,128]{2,0,1:T(8,128)S(1)}, f32[80,8,128]{2,0,1:T(8,128)S(1)}, u32[]{:S(2)}, u32[]{:S(2)}) collective-permute-start(f32[80,8,128]{2,0,1:T(8,128)S(1)} %get-tuple-element.14), channel_id=1, source_target_pairs={{1,0},{3,2},{5,4},{7,6},{9,8},{11,10},{13,12},{15,14},{17,16},{19,... | collective-permute-start | bytes 983048 | tf_op jit(solution)/shard_map/ppermute | solution.py:44
  55.1 15.5 %collective-permute-start.9 = (f32[80,8,128]{2,0,1:T(8,128)S(1)}, f32[80,8,128]{2,0,1:T(8,128)S(1)}, u32[]{:S(2)}, u32[]{:S(2)}) collective-permute-start(f32[80,8,128]{2,0,1:T(8,128)S(1)} %get-tuple-element.13), channel_id=1, source_target_pairs={{0,1},{2,3},{4,5},{6,7},{8,9},{10,11},{12,13},{14,15},{16,17},{18,... | collective-permute-start | bytes 983048 | tf_op jit(solution)/shard_map/ppermute | solution.py:41
  76.8 3.6 %collective-permute-start.11 = (f32[8,16,128]{2,1,0:T(8,128)S(1)}, f32[8,16,128]{2,1,0:T(8,128)S(1)}, u32[]{:S(2)}, u32[]{:S(2)}) collective-permute-start(f32[8,16,128]{2,1,0:T(8,128)S(1)} %get-tuple-element.15), channel_id=1, source_target_pairs={{0,2},{2,4},{4,6},{1,3},{3,5},{5,7},{8,10},{10,12},{12,14},{9,11},... | collective-permute-start | bytes 196616 | tf_op jit(solution)/shard_map/ppermute | solution.py:41
  78.5 6.2 %collective-permute-start.12 = (f32[8,16,128]{2,1,0:T(8,128)S(1)}, f32[8,16,128]{2,1,0:T(8,128)S(1)}, u32[]{:S(2)}, u32[]{:S(2)}) collective-permute-start(f32[8,16,128]{2,1,0:T(8,128)S(1)} %get-tuple-element.16), channel_id=1, source_target_pairs={{2,0},{4,2},{6,4},{3,1},{5,3},{7,5},{10,8},{12,10},{14,12},{11,9},... | collective-permute-start | bytes 196616 | tf_op jit(solution)/shard_map/ppermute | solution.py:44
  84.8 7.3 %collective-permute-start.13 = (f32[80,8,128]{2,1,0:T(8,128)S(1)}, f32[80,8,128]{2,1,0:T(8,128)S(1)}, u32[]{:S(2)}, u32[]{:S(2)}) collective-permute-start(f32[80,8,128]{2,1,0:T(8,128)S(1)} %get-tuple-element.11), channel_id=1, source_target_pairs={{0,1},{2,3},{4,5},{6,7},{8,9},{10,11},{12,13},{14,15},{16,17},{18,... | collective-permute-start | bytes 983048 | tf_op jit(solution)/shard_map/ppermute | solution.py:41
  87.5 9.0 %collective-permute-start.14 = (f32[80,8,128]{2,1,0:T(8,128)S(1)}, f32[80,8,128]{2,1,0:T(8,128)S(1)}, u32[]{:S(2)}, u32[]{:S(2)}) collective-permute-start(f32[80,8,128]{2,1,0:T(8,128)S(1)} %get-tuple-element.12), channel_id=1, source_target_pairs={{1,0},{3,2},{5,4},{7,6},{9,8},{11,10},{13,12},{15,14},{17,16},{19,... | collective-permute-start | bytes 983048 | tf_op jit(solution)/shard_map/ppermute | solution.py:44
Sparse Core Ops, SparseCore 0:
  101.1 32.7 all-reduce.1
